TPU v7x, 256 devices: a whole 4x4x8 slice. The times are simulated.
256 devices in a mesh: ctx: 32 (over z, y), tp: 8 (over x, core).
Axes of the slice: x: 4, y: 4, z: 8, core: 2. Of those that a mesh axis runs over, the one named last changes fastest.
Arguments:
- tokens: bfloat16 [24576, 4096], P(('ctx', 'tp')), may hold values from -6 to 6
- norm_gain: float32 [4096], replicated, may hold values from 0.1 to 1.9
- w_qkv: bfloat16 [4096, 8192], P('ctx', 'tp'), may hold values from -0.09375 to 0.09375
- w_out: bfloat16 [4096, 4096], P('tp', 'ctx'), may hold values from -0.09375 to 0.09375
- head_gain: float32 [4096], P('tp'), may hold values from 0.1 to 1.9
- input_codes: int32 [8, 24576], P('tp', 'ctx'), may hold values from -4 to 4
- forget_codes: int32 [8, 24576], P('tp', 'ctx'), may hold values from -24 to 4
- forget_bias: float32 [8], P('tp'), may hold values from 3 to 13.5, as said below
- document_begin_flags: int32 [24576], P('ctx'), may hold values 0 or 1
Outputs:
- mixed: bfloat16 [24576, 4096], P(('ctx', 'tp'))
Inputs may be any that keep to these rules, and one draw needn't show every extreme that they name: `forget_bias`: a bias for each head.
All inputs are finite; a program needn't handle non-finite values. No bound on the sum of `document_begin_flags` on one device may be relied on, other than what follows from the above.
Results may differ from a plain program's by a relative error of at most 0.017.
Values may be sent and summed in bfloat16 or wider, within the bound.
A program may use at most 64 MiB of HBM per device.

v0:
```python
import jax
import jax.numpy as jnp
from jax import lax
from jax.sharding import PartitionSpec as P

DK = 256
DV = 512
EPSILON = 1e-06
FORGET_STEP = 0.5
INPUT_STEP = 0.5


def carried_in(shard, axis, combine, identity):
    count, position = (lax.axis_size(axis), lax.axis_index(axis))
    everything = jax.tree.map(
        lambda part, kind: lax.all_gather(part.astype(kind), axis),
        shard,
        (jnp.bfloat16, jnp.bfloat16),
    )
    start = jax.tree.map(
        lambda part, zero: jnp.broadcast_to(jnp.asarray(zero, part.dtype), part.shape),
        shard,
        identity,
    )

    def hop(k, before):
        reached = k < position
        new = combine(
            before, jax.tree.map(lambda part, own: part[k].astype(own.dtype), everything, shard)
        )
        return jax.tree.map(lambda a, b: jnp.where(reached, a, b), new, before)

    return lax.fori_loop(0, count, hop, start)


def rms_rows(embedded_entries, norm_gain):
    token_float = embedded_entries.astype(jnp.float32)
    moment = jnp.mean(token_float * token_float, axis=1, keepdims=True)
    return (token_float * lax.rsqrt(moment + EPSILON) * norm_gain).astype(jnp.bfloat16)


def local_terms(queries, key_rows, values, log_forget, input_gate, starts):
    length = queries.shape[0]
    scaling = queries.shape[1] ** (-0.5)
    segment = jnp.cumsum(starts)
    levels = jnp.cumsum(log_forget)
    position = jnp.arange(length)
    allowed = (position[:, None] >= position[None, :]) & (segment[:, None] == segment[None, :])
    decays = jnp.where(
        allowed,
        jnp.exp(jnp.minimum(levels[:, None] - levels[None, :], 0.0) + input_gate[None, :]),
        0.0,
    )
    scores = jnp.dot(queries, key_rows.T, preferred_element_type=jnp.float32) * scaling
    weights = (scores * decays).astype(jnp.bfloat16)
    inner_part = jnp.dot(weights, values, preferred_element_type=jnp.float32)
    last_level = levels[-1]
    last_seg = segment[-1]
    keeping = jnp.where(segment == last_seg, jnp.exp(last_level - levels + input_gate), 0.0)
    weighted = (key_rows.astype(jnp.float32) * keeping[:, None]).astype(jnp.bfloat16)
    local_state = lax.dot_general(
        weighted, values, (((0,), (0,)), ((), ())), preferred_element_type=jnp.float32
    )
    passing = jnp.where(last_seg == 0, jnp.exp(last_level), 0.0)
    carried = jnp.where(segment == 0, jnp.exp(levels), 0.0) * scaling
    return (inner_part, local_state, passing, carried)


def apply_state(queries, carried, incoming):
    lifted = queries.astype(jnp.float32) * carried[:, None]
    return jnp.dot(
        lifted, incoming, precision=lax.Precision.HIGHEST, preferred_element_type=jnp.float32
    )


def head_norm(head_out, gain):
    centre = jnp.mean(head_out, axis=1, keepdims=True)
    shifted = head_out - centre
    spread = jnp.mean(shifted * shifted, axis=1, keepdims=True)
    return (shifted * lax.rsqrt(spread + EPSILON) * gain).astype(jnp.bfloat16)


def combine(earlier, later):
    return (earlier[0] * later[0], later[0][:, None, None] * earlier[1] + later[1])


def local(
    tokens,
    norm_gain,
    w_qkv,
    w_out,
    head_gain,
    input_codes,
    forget_codes,
    forget_bias,
    document_begin_flags,
):
    normed = rms_rows(tokens, norm_gain)
    every_row_list = lax.all_gather(normed, "tp", axis=0, tiled=True)
    parameter_collection = lax.all_gather(w_qkv, "ctx", axis=0, tiled=True)
    rows_combined = jnp.dot(
        every_row_list, parameter_collection, preferred_element_type=jnp.float32
    )
    rows_combined = rows_combined.astype(jnp.bfloat16)
    heads_here = forget_bias.shape[0]
    stride = 2 * DK + DV
    query_list, inner_list, state_list, passing_list, carried_list = ([], [], [], [], [])
    attention_slot_number = 0
    offset = attention_slot_number * stride
    queries = rows_combined[:, offset : offset + DK]
    key_rows = rows_combined[:, offset + DK : offset + 2 * DK]
    values = rows_combined[:, offset + 2 * DK : offset + stride]
    log_forget = jax.nn.log_sigmoid(
        FORGET_STEP * forget_codes[attention_slot_number].astype(jnp.float32)
        + forget_bias[attention_slot_number]
    )
    input_gate = INPUT_STEP * input_codes[attention_slot_number].astype(jnp.float32)
    inner_part, local_state, passing, carried = local_terms(
        queries, key_rows, values, log_forget, input_gate, document_begin_flags
    )
    query_list.append(queries)
    inner_list.append(inner_part)
    state_list.append(local_state)
    passing_list.append(passing)
    carried_list.append(carried)
    identity = (jnp.ones((heads_here,), jnp.float32), jnp.zeros((heads_here, DK, DV), jnp.float32))
    scanned = carried_in((jnp.stack(passing_list), jnp.stack(state_list)), "ctx", combine, identity)
    incoming = scanned[1]
    attention_slot_number = 0
    head_out = inner_list[attention_slot_number] + apply_state(
        query_list[attention_slot_number],
        carried_list[attention_slot_number],
        incoming[attention_slot_number],
    )
    normed_heads = head_norm(head_out, head_gain)
    out_columns = lax.all_gather(w_out, "ctx", axis=1, tiled=True)
    summed = lax.psum_scatter(
        jnp.dot(normed_heads, out_columns, preferred_element_type=jnp.float32).astype(jnp.bfloat16),
        "tp",
        scatter_dimension=0,
        tiled=True,
    ).astype(jnp.float32)
    return (tokens.astype(jnp.float32) + summed).astype(jnp.bfloat16)


def solution(mesh):
    placed = (
        P(("ctx", "tp"), None),
        P(),
        P("ctx", "tp"),
        P("tp", "ctx"),
        P("tp"),
        P("tp", "ctx"),
        P("tp", "ctx"),
        P("tp"),
        P("ctx"),
    )
    return jax.shard_map(
        local, mesh=mesh, in_specs=placed, out_specs=P(("ctx", "tp"), None), check_vma=False
    )
```

profile of v0, /device:TPU:1, one launch (start us, length us, event | category | flops | bytes accessed | tf_op | source)
XLA Modules:
  0.0 411.1 jit_solution(12727475956866767131)
XLA Ops:
  6.5 1.4 fusion.2
  8.0 2.3 fusion.4
  14.2 1.3 exponential_select_fusion
  15.5 42.6 %all-gather.6.cloned.1.call-done = bf16[768,4096]{1,0:T(8,128)(2,1)} async-done(((bf16[96,4096]{1,0:T(8,128)(2,1)}), bf16[768,4096]{1,0:T(8,128)(2,1)}) %all-gather.6.cloned.1.call-update) | async-done | bytes 6291472 | tf_op jit(solution)/shard_map/all_gather | solution.py:99
  58.1 100.4 %all-gather.8.cloned.1.call-done = bf16[4096,1024]{1,0:T(8,128)(2,1)} async-done(((bf16[128,1024]{1,0:T(8,128)(2,1)}), bf16[4096,1024]{1,0:T(8,128)(2,1)}) %all-gather.8.cloned.1.call-update) | async-done | bytes 8388624 | tf_op jit(solution)/shard_map/all_gather | solution.py:100
  158.5 10.9 %convolution_convert_fusion.1 = bf16[768,1024]{1,0:T(8,128)(2,1)S(1)} fusion(bf16[768,4096]{1,0:T(8,128)(2,1)} %all-gather.6.cloned.1.call-done, bf16[4096,1024]{1,0:T(8,128)(2,1)} %all-gather.8.cloned.1.call-done), kind=kOutput, calls=%fused_computation.10 | convolution fusion | flops 6443237376 | bytes 16252928 | tf_op jit(solution)/shard_map/dot_general | solution.py:101
  169.5 1.3 convolution_convert_fusion.2
  174.2 57.4 %all-reduce = bf16[32]{0:T(256)(128)(2,1)S(1)} all-reduce(bf16[32]{0:T(256)(128)(2,1)S(1)} %dynamic-update-slice), channel_id=1, replica_groups=mesh['ctx'=32,'tp'=8] {'ctx'}, use_global_device_ids=true, to_apply=%add | all-reduce | flops 32 | bytes 128
  231.6 2.5 fusion.6
  234.2 32.5 %all-gather.12.cloned.1.call-done = bf16[8192,512]{1,0:T(8,128)(2,1)} async-done(((bf16[256,512]{1,0:T(8,128)(2,1)}), bf16[8192,512]{1,0:T(8,128)(2,1)}) %all-gather.12.cloned.1.call-update) | async-done | bytes 8388624 | tf_op jit(solution)/shard_map/all_gather | solution.py:16
  266.7 81.1 %while.14 = (s32[]{:T(128)}, f32[1,256,512]{2,1,0:T(8,128)S(1)}, s32[]{:T(128)}, bf16[32,1]{0,1:T(2,128)(2,1)S(1)}, bf16[32,1,256,512]{3,2,1,0:T(8,128)(2,1)}, /*index=5*/s32[]{:T(128)}, s32[]{:T(128)}) while((s32[]{:T(128)}, f32[1,256,512]{2,1,0:T(8,128)S(1)}, s32[]{:T(128)}, bf16[32,1]{0,1:T(2,128)(2,1)S(1)}, ...), condition=%wide.region_6.7_spmd.clone, body=%wide.region_5.6_spmd.clone.sunk | while | flops 655365 | bytes 1310839 | solution.py:33
  267.9 1.3 fusion.42
  270.5 1.3 fusion.42
  273.0 1.3 fusion.42
  275.5 1.3 fusion.42
  278.1 1.3 fusion.42
  280.6 1.3 fusion.42
  283.1 1.3 fusion.42
  285.7 1.3 fusion.42
  288.2 1.3 fusion.42
  290.7 1.3 fusion.42
  293.3 1.3 fusion.42
  295.8 1.3 fusion.42
  311.0 1.3 fusion.42
  316.1 1.3 fusion.42
  326.2 1.3 fusion.42
  331.3 1.3 fusion.42
  344.0 1.3 fusion.42
  347.8 3.2 fusion.37
  351.7 7.7 %convolution_convert_fusion = bf16[768,4096]{1,0:T(8,128)(2,1)} fusion(bf16[512,4096]{1,0:T(8,128)(2,1)} %all-gather.10.cloned.1.call-done, f32[768,512]{0,1:T(8,128)S(1)} %get-tuple-element.142, f32[512]{0:T(512)S(1)} %copy-done.5, f32[768]{0:T(1024)S(1)} %add_rsqrt_fusion, f32[768]{0:T(1024)S(1)} %broadcast_multiply_fusion), kind=kOutput, calls=%fused_computation.3 | convolution fusion | flops 3225944064 | bytes 12066816 | tf_op jit(solution)/shard_map/dot_general | solution.py:138
  359.5 42.9 %reduce-scatter.2.cloned.1.call-done = bf16[96,4096]{1,0:T(8,128)(2,1)} async-done(((bf16[768,4096]{1,0:T(8,128)(2,1)}), bf16[96,4096]{1,0:T(8,128)(2,1)}) %reduce-scatter.2.cloned.1.call-update) | async-done | bytes 786448 | tf_op jit(solution)/shard_map/reduce_scatter | solution.py:137
  402.4 2.2 fusion.5
  (94 shorter events, 43.7 us)
Async XLA Ops:
  6.5 5.2 %copy-start.4 = (s32[1,768]{1,0:T(1,128)S(1)}, s32[1,768]{1,0:T(1,128)}, u32[]{:S(2)}) copy-start(s32[1,768]{1,0:T(1,128)} %param.17) | copy-start | bytes 9220
  6.5 5.6 %copy-start.2 = (s32[768]{0:T(1024)S(1)}, s32[768]{0:T(1024)}, u32[]{:S(2)}) copy-start(s32[768]{0:T(1024)} %param.19) | copy-start | bytes 9220
  6.5 51.6 %all-gather.6.cloned.1.call-start = ((), (), s32[]{:S(2)}) async-start(), calls=%async_computation.1 | async-start | bytes 7077888 | tf_op jit(solution)/shard_map/all_gather | solution.py:99
  8.0 6.2 %copy-start.3 = (s32[1,768]{1,0:T(1,128)S(1)}, s32[1,768]{1,0:T(1,128)}, u32[]{:S(2)}) copy-start(s32[1,768]{1,0:T(1,128)} %param.16) | copy-start | bytes 9220
  10.3 148.3 %all-gather.8.cloned.1.call-start = ((), (), s32[]{:S(2)}) async-start(), calls=%async_computation.2 | async-start | bytes 8650752 | tf_op jit(solution)/shard_map/all_gather | solution.py:100
  11.0 255.7 %all-gather.12.cloned.1.call-start = ((), (), s32[]{:S(2)}) async-start(), calls=%async_computation.5 | async-start | bytes 8650752 | tf_op jit(solution)/shard_map/all_gather | solution.py:16
  169.5 64.7 %copy-start.1 = (bf16[768,1024]{1,0:T(8,128)(2,1)}, bf16[768,1024]{1,0:T(8,128)(2,1)S(1)}, u32[]{:S(2)}) copy-start(bf16[768,1024]{1,0:T(8,128)(2,1)S(1)} %convolution_convert_fusion.1) | copy-start | bytes 4718596
  169.5 3.3 copy-start.6
  170.8 180.5 %all-gather.10.cloned.1.call-start = ((), (), s32[]{:S(2)}) async-start(), calls=%async_computation.3 | async-start | bytes 4325376 | tf_op jit(solution)/shard_map/all_gather | solution.py:136
  171.4 231.0 %reduce-scatter.2.cloned.1.call-start = ((), (), s32[]{:S(2)}) async-start(), calls=%async_computation.4 | async-start | bytes 7077888 | tf_op jit(solution)/shard_map/reduce_scatter | solution.py:137
  351.0 0.7 copy-start.5
  359.4 42.9 %copy-start = (bf16[96,4096]{1,0:T(8,128)(2,1)S(1)}, bf16[96,4096]{1,0:T(8,128)(2,1)}, u32[]{:S(2)}) copy-start(bf16[96,4096]{1,0:T(8,128)(2,1)} %param.11) | copy-start | bytes 2359300
Sparse Core Ops, SparseCore 0:
  10.4 47.6 all-gather.5
  60.7 97.8 all-gather.7
  170.9 95.7 all-gather.11
  269.0 77.5 all-gather.9
  359.6 42.7 reduce-scatter.1
where the time goes:
time: 413 us; the launch traced here: 411 us
  waiting for transfers between devices  220 us (53%)
  blocking collectives  57.4 us (14%)
  other arithmetic  48.8 us (12%)
  matrix products  25.7 us (6%)
  local copies, waits for them, and re-layouts  22.3 us (5%)
  loops' own time  21.7 us (5%)
  between operations  15.3 us (4%)
    all_gather x1, waiting for transfers between devices, local(): parameter_collection = lax.all_gather(w_qkv, 'ctx', axis=0, tiled=True)  100 us
    unnamed x1, blocking collectives  57.4 us
    reduce_scatter x1, waiting for transfers between devices, local(): lax.psum_scatter(jnp.dot(normed_heads, out_columns, preferred_element_typ...  42.9 us
    all_gather x1, waiting for transfers between devices, local(): every_row_list = lax.all_gather(normed, 'tp', axis=0, tiled=True)  42.6 us
    select_n x32, other arithmetic, hop(): return jax.tree.map(lambda a, b: jnp.where(reached, a, b), new, before)  40.6 us
    all_gather x1, waiting for transfers between devices, carried_in(): lax.all_gather(part.astype(kind), axis)  32.5 us
    another operation x1, loops' own time, carried_in(): return lax.fori_loop(0, count, hop, start)  21.7 us
    dynamic_slice x32, local copies, waits for them, and re-layouts, hop(): part[k].astype(own.dtype)  18.7 us
  transfers between devices with their start and end apart: 5, of which 4 were waited for; matrix products, arithmetic and copies ran while one was open for 17% of the time, Pallas kernels for 0%

commit v1 on v0

--- a/solution.py
+++ b/solution.py
@@ -96,7 +96,14 @@
     document_begin_flags,
 ):
     normed = rms_rows(tokens, norm_gain)
-    every_row_list = lax.all_gather(normed, "tp", axis=0, tiled=True)
+    peers = lax.axis_size("tp")
+    route = [(i, (i + 1) % peers) for i in range(peers)]
+    parts = [normed]
+    for far in range(1, peers):
+        parts = [lax.ppermute(parts[0], "tp", route), *parts]
+    out = jnp.concatenate(parts, axis=0)
+    offset_2 = (lax.axis_index("tp") + 1) * parts[-1].shape[0]
+    every_row_list = jnp.roll(out, offset_2, axis=0)
     parameter_collection = lax.all_gather(w_qkv, "ctx", axis=0, tiled=True)
     rows_combined = jnp.dot(
         every_row_list, parameter_collection, preferred_element_type=jnp.float32

time: 413 us -> 380 us (0.920)
  waiting for transfers between devices: 220 us -> 142 us
  local copies, waits for them, and re-layouts: 22.3 us -> 42.1 us
  starting transfers between devices: 0.16 us -> 17.7 us
  blocking collectives: 57.4 us -> 63.8 us
    all_gather x1, waiting for transfers between devices: 100 us -> 0.01 us  [local(): parameter_collection = lax.all_gather(w_qkv, 'ctx', axis=0, tiled=True)]
    ppermute x0 -> x7, waiting for transfers between devices: none -> 59.7 us  [local(): parts = [lax.ppermute(parts[0], 'tp', route), *parts]]
    all_gather x1 -> x0, waiting for transfers between devices: 42.6 us -> none  [local(): every_row_list = lax.all_gather(normed, 'tp', axis=0, tiled=True)]
    unnamed x17 -> x37, local copies, waits for them, and re-layouts: 1.84 us -> 21.7 us
    ppermute x0 -> x7, starting transfers between devices: none -> 17.6 us  [local(): parts = [lax.ppermute(parts[0], 'tp', route), *parts]]
    unnamed x1, blocking collectives: 57.4 us -> 63.8 us
    all_gather x1, waiting for transfers between devices: 32.5 us -> 37.4 us  [carried_in(): lax.all_gather(part.astype(kind), axis)]
  transfers between devices with their start and end apart: 5 -> 11, of which waited for: 4 -> 9; matrix products, arithmetic and copies ran while one was open for 17% -> 25% of each run, Pallas kernels for 0% -> 0%
where the time goes in v1:
time: 380 us; the launch traced here: 378 us
  waiting for transfers between devices  142 us (37%)
  blocking collectives  63.8 us (17%)
  other arithmetic  50.2 us (13%)
  local copies, waits for them, and re-layouts  42.1 us (11%)
  matrix products  25.7 us (7%)
  loops' own time  21.7 us (6%)
  starting transfers between devices  17.7 us (5%)
  between operations  15.3 us (4%)
    unnamed x1, blocking collectives  63.8 us
    ppermute x7, waiting for transfers between devices, local(): parts = [lax.ppermute(parts[0], 'tp', route), *parts]  59.7 us
    reduce_scatter x1, waiting for transfers between devices, local(): lax.psum_scatter(jnp.dot(normed_heads, out_columns, preferred_element_typ...  43.4 us
    select_n x32, other arithmetic, hop(): return jax.tree.map(lambda a, b: jnp.where(reached, a, b), new, before)  40.6 us
    all_gather x1, waiting for transfers between devices, carried_in(): lax.all_gather(part.astype(kind), axis)  37.4 us
    another operation x1, loops' own time, carried_in(): return lax.fori_loop(0, count, hop, start)  21.7 us
    unnamed x37, local copies, waits for them, and re-layouts  21.7 us
    dynamic_slice x32, local copies, waits for them, and re-layouts, hop(): part[k].astype(own.dtype)  18.7 us
  transfers between devices with their start and end apart: 11, of which 9 were waited for; matrix products, arithmetic and copies ran while one was open for 25% of the time, Pallas kernels for 0%

profile of v1, /device:TPU:1, one launch (start us, length us, event | category | flops | bytes accessed | tf_op | source)
XLA Modules:
  0.0 378.4 jit_solution(820193846971510509)
XLA Ops:
  7.3 1.4 fusion.7
  8.7 1.4 fusion.9
  10.1 2.6 collective-permute-start
  12.7 8.9 %collective-permute-done = bf16[96,4096]{1,0:T(8,128)(2,1)S(1)} collective-permute-done((bf16[96,4096]{1,0:T(8,128)(2,1)S(1)}, bf16[96,4096]{1,0:T(8,128)(2,1)S(1)}, u32[]{:S(2)}, u32[]{:S(2)}) %collective-permute-start) | collective-permute-done | bytes 786464 | tf_op jit(solution)/shard_map/ppermute | solution.py:103
  21.7 2.5 collective-permute-start.1
  24.1 8.9 %collective-permute-done.1 = bf16[96,4096]{1,0:T(8,128)(2,1)S(1)} collective-permute-done((bf16[96,4096]{1,0:T(8,128)(2,1)S(1)}, bf16[96,4096]{1,0:T(8,128)(2,1)S(1)}, u32[]{:S(2)}, u32[]{:S(2)}) %collective-permute-start.1) | collective-permute-done | bytes 786464 | tf_op jit(solution)/shard_map/ppermute | solution.py:103
  33.1 2.5 collective-permute-start.2
  35.6 8.9 %collective-permute-done.2 = bf16[96,4096]{1,0:T(8,128)(2,1)S(1)} collective-permute-done((bf16[96,4096]{1,0:T(8,128)(2,1)S(1)}, bf16[96,4096]{1,0:T(8,128)(2,1)S(1)}, u32[]{:S(2)}, u32[]{:S(2)}) %collective-permute-start.2) | collective-permute-done | bytes 786464 | tf_op jit(solution)/shard_map/ppermute | solution.py:103
  44.5 2.5 collective-permute-start.3
  47.0 8.9 %collective-permute-done.3 = bf16[96,4096]{1,0:T(8,128)(2,1)S(1)} collective-permute-done((bf16[96,4096]{1,0:T(8,128)(2,1)S(1)}, bf16[96,4096]{1,0:T(8,128)(2,1)S(1)}, u32[]{:S(2)}, u32[]{:S(2)}) %collective-permute-start.3) | collective-permute-done | bytes 786464 | tf_op jit(solution)/shard_map/ppermute | solution.py:103
  55.9 2.5 collective-permute-start.4
  58.4 8.9 %collective-permute-done.4 = bf16[96,4096]{1,0:T(8,128)(2,1)} collective-permute-done((bf16[96,4096]{1,0:T(8,128)(2,1)S(1)}, bf16[96,4096]{1,0:T(8,128)(2,1)}, u32[]{:S(2)}, u32[]{:S(2)}) %collective-permute-start.4) | collective-permute-done | bytes 786464 | tf_op jit(solution)/shard_map/ppermute | solution.py:103
  67.3 2.6 collective-permute-start.5
  71.0 8.2 %collective-permute-done.5 = bf16[96,4096]{1,0:T(8,128)(2,1)} collective-permute-done((bf16[96,4096]{1,0:T(8,128)(2,1)}, bf16[96,4096]{1,0:T(8,128)(2,1)}, u32[]{:S(2)}, u32[]{:S(2)}) %collective-permute-start.5) | collective-permute-done | bytes 786464 | tf_op jit(solution)/shard_map/ppermute | solution.py:103
  79.2 2.5 collective-permute-start.6
  84.9 6.8 %collective-permute-done.6 = bf16[96,4096]{1,0:T(8,128)(2,1)} collective-permute-done((bf16[96,4096]{1,0:T(8,128)(2,1)}, bf16[96,4096]{1,0:T(8,128)(2,1)}, u32[]{:S(2)}, u32[]{:S(2)}) %collective-permute-start.6) | collective-permute-done | bytes 786464 | tf_op jit(solution)/shard_map/ppermute | solution.py:103
  91.7 2.1 constant_dynamic-update-slice_fusion.15
  93.8 2.1 constant_dynamic-update-slice_fusion.14
  95.9 2.1 constant_dynamic-update-slice_fusion.13
  103.0 2.2 constant_dynamic-update-slice_fusion.7
  105.1 2.1 constant_dynamic-update-slice_fusion.6
  107.2 2.1 constant_dynamic-update-slice_fusion.5
  114.3 11.0 %fusion.4 = bf16[768,1024]{1,0:T(8,128)(2,1)S(1)} fusion(bf16[4096,1024]{1,0:T(8,128)(2,1)} %all-gather.5.cloned.1.call-done, bf16[1536,4096]{1,0:T(8,128)(2,1)} %constant_dynamic-update-slice_fusion, s32[]{:T(128)S(6)} %select_n.65), kind=kOutput, calls=%fused_computation.12 | convolution fusion | flops 6443237376 | bytes 16252932 | tf_op jit(solution)/shard_map/dot_general | solution.py:108
  130.1 63.8 %all-reduce = bf16[32]{0:T(256)(128)(2,1)S(1)} all-reduce(bf16[32]{0:T(256)(128)(2,1)S(1)} %dynamic-update-slice), channel_id=1, replica_groups=mesh['ctx'=32,'tp'=8] {'ctx'}, use_global_device_ids=true, to_apply=%add | all-reduce | flops 32 | bytes 128
  193.9 2.5 fusion.11
  196.5 37.4 %all-gather.9.cloned.1.call-done = bf16[8192,512]{1,0:T(8,128)(2,1)} async-done(((bf16[256,512]{1,0:T(8,128)(2,1)}), bf16[8192,512]{1,0:T(8,128)(2,1)}) %all-gather.9.cloned.1.call-update) | async-done | bytes 8388624 | tf_op jit(solution)/shard_map/all_gather | solution.py:16
  233.9 81.1 %while.14 = (s32[]{:T(128)}, f32[1,256,512]{2,1,0:T(8,128)S(1)}, s32[]{:T(128)}, bf16[32,1]{0,1:T(2,128)(2,1)S(1)}, bf16[32,1,256,512]{3,2,1,0:T(8,128)(2,1)}, /*index=5*/s32[]{:T(128)}, s32[]{:T(128)}) while((s32[]{:T(128)}, f32[1,256,512]{2,1,0:T(8,128)S(1)}, s32[]{:T(128)}, bf16[32,1]{0,1:T(2,128)(2,1)S(1)}, ...), condition=%wide.region_6.7_spmd.clone, body=%wide.region_5.6_spmd.clone.sunk | while | flops 655365 | bytes 1310839 | solution.py:33
  298.5 1.3 fusion.47
  315.0 3.2 fusion.43
  318.4 7.8 %convolution_convert_fusion = bf16[768,4096]{1,0:T(8,128)(2,1)} fusion(bf16[512,4096]{1,0:T(8,128)(2,1)} %all-gather.7.cloned.1.call-done, f32[768,512]{0,1:T(8,128)S(1)} %get-tuple-element.142, f32[512]{0:T(512)S(1)} %copy-done.8, f32[768]{0:T(1024)S(1)} %add_rsqrt_fusion, f32[768]{0:T(1024)S(1)} %broadcast_multiply_fusion), kind=kOutput, calls=%fused_computation.3 | convolution fusion | flops 3225944064 | bytes 12066816 | tf_op jit(solution)/shard_map/dot_general | solution.py:145
  326.2 43.4 %reduce-scatter.2.cloned.1.call-done = bf16[96,4096]{1,0:T(8,128)(2,1)} async-done(((bf16[768,4096]{1,0:T(8,128)(2,1)}), bf16[96,4096]{1,0:T(8,128)(2,1)}) %reduce-scatter.2.cloned.1.call-update) | async-done | bytes 786448 | tf_op jit(solution)/shard_map/reduce_scatter | solution.py:144
  369.6 2.2 fusion.10
  (127 shorter events, 76.2 us)
Async XLA Ops:
  6.5 64.0 %copy-start.7 = (s32[1,768]{1,0:T(1,128)S(1)}, s32[1,768]{1,0:T(1,128)}, u32[]{:S(2)}) copy-start(s32[1,768]{1,0:T(1,128)} %param.17) | copy-start | bytes 9220
  6.5 75.1 %copy-start.5 = (s32[768]{0:T(1024)S(1)}, s32[768]{0:T(1024)}, u32[]{:S(2)}) copy-start(s32[768]{0:T(1024)} %param.19) | copy-start | bytes 9220
  6.5 77.1 %copy-start.6 = (s32[1,768]{1,0:T(1,128)S(1)}, s32[1,768]{1,0:T(1,128)}, u32[]{:S(2)}) copy-start(s32[1,768]{1,0:T(1,128)} %param.16) | copy-start | bytes 9220
  6.5 107.8 %all-gather.5.cloned.1.call-start = ((), (), s32[]{:S(2)}) async-start(), calls=%async_computation.1 | async-start | bytes 8650752 | tf_op jit(solution)/shard_map/all_gather | solution.py:107
  7.3 226.6 %all-gather.9.cloned.1.call-start = ((), (), s32[]{:S(2)}) async-start(), calls=%async_computation.4 | async-start | bytes 8650752 | tf_op jit(solution)/shard_map/all_gather | solution.py:16
  10.1 11.5 %collective-permute-start = (bf16[96,4096]{1,0:T(8,128)(2,1)S(1)}, bf16[96,4096]{1,0:T(8,128)(2,1)S(1)}, u32[]{:S(2)}, u32[]{:S(2)}) collective-permute-start(bf16[96,4096]{1,0:T(8,128)(2,1)S(1)} %fusion.9), channel_id=1, source_target_pairs={{0,1},{1,2},{2,3},{3,4},{4,5},{5,6},{6,7},{7,0},{8,9},{9,10},{10,1... | collective-permute-start | bytes 2359304 | tf_op jit(solution)/shard_map/ppermute | solution.py:103
  21.7 11.4 %collective-permute-start.1 = (bf16[96,4096]{1,0:T(8,128)(2,1)S(1)}, bf16[96,4096]{1,0:T(8,128)(2,1)S(1)}, u32[]{:S(2)}, u32[]{:S(2)}) collective-permute-start(bf16[96,4096]{1,0:T(8,128)(2,1)S(1)} %collective-permute-done), channel_id=1, source_target_pairs={{0,1},{1,2},{2,3},{3,4},{4,5},{5,6},{6,7},{7,0},{8,9},{9,10},{10,1... | collective-permute-start | bytes 2359304 | tf_op jit(solution)/shard_map/ppermute | solution.py:103
  33.1 11.4 %collective-permute-start.2 = (bf16[96,4096]{1,0:T(8,128)(2,1)S(1)}, bf16[96,4096]{1,0:T(8,128)(2,1)S(1)}, u32[]{:S(2)}, u32[]{:S(2)}) collective-permute-start(bf16[96,4096]{1,0:T(8,128)(2,1)S(1)} %collective-permute-done.1), channel_id=1, source_target_pairs={{0,1},{1,2},{2,3},{3,4},{4,5},{5,6},{6,7},{7,0},{8,9},{9,10},{10,1... | collective-permute-start | bytes 2359304 | tf_op jit(solution)/shard_map/ppermute | solution.py:103
  44.5 11.4 %collective-permute-start.3 = (bf16[96,4096]{1,0:T(8,128)(2,1)S(1)}, bf16[96,4096]{1,0:T(8,128)(2,1)S(1)}, u32[]{:S(2)}, u32[]{:S(2)}) collective-permute-start(bf16[96,4096]{1,0:T(8,128)(2,1)S(1)} %collective-permute-done.2), channel_id=1, source_target_pairs={{0,1},{1,2},{2,3},{3,4},{4,5},{5,6},{6,7},{7,0},{8,9},{9,10},{10,1... | collective-permute-start | bytes 2359304 | tf_op jit(solution)/shard_map/ppermute | solution.py:103
  55.9 42.1 %copy-start.1 = (bf16[96,4096]{1,0:T(8,128)(2,1)}, bf16[96,4096]{1,0:T(8,128)(2,1)S(1)}, u32[]{:S(2)}) copy-start(bf16[96,4096]{1,0:T(8,128)(2,1)S(1)} %collective-permute-done.3) | copy-start | bytes 2359300
  55.9 11.4 %collective-permute-start.4 = (bf16[96,4096]{1,0:T(8,128)(2,1)S(1)}, bf16[96,4096]{1,0:T(8,128)(2,1)}, u32[]{:S(2)}, u32[]{:S(2)}) collective-permute-start(bf16[96,4096]{1,0:T(8,128)(2,1)S(1)} %collective-permute-done.3), channel_id=1, source_target_pairs={{0,1},{1,2},{2,3},{3,4},{4,5},{5,6},{6,7},{7,0},{8,9},{9,10},{10,1... | collective-permute-start | bytes 2359304 | tf_op jit(solution)/shard_map/ppermute | solution.py:103
  67.3 11.8 %collective-permute-start.5 = (bf16[96,4096]{1,0:T(8,128)(2,1)}, bf16[96,4096]{1,0:T(8,128)(2,1)}, u32[]{:S(2)}, u32[]{:S(2)}) collective-permute-start(bf16[96,4096]{1,0:T(8,128)(2,1)} %collective-permute-done.4), channel_id=1, source_target_pairs={{0,1},{1,2},{2,3},{3,4},{4,5},{5,6},{6,7},{7,0},{8,9},{9,10},{10,1... | collective-permute-start | bytes 2359304 | tf_op jit(solution)/shard_map/ppermute | solution.py:103
  79.2 12.5 %collective-permute-start.6 = (bf16[96,4096]{1,0:T(8,128)(2,1)}, bf16[96,4096]{1,0:T(8,128)(2,1)}, u32[]{:S(2)}, u32[]{:S(2)}) collective-permute-start(bf16[96,4096]{1,0:T(8,128)(2,1)} %collective-permute-done.5), channel_id=1, source_target_pairs={{0,1},{1,2},{2,3},{3,4},{4,5},{5,6},{6,7},{7,0},{8,9},{9,10},{10,1... | collective-permute-start | bytes 2359304 | tf_op jit(solution)/shard_map/ppermute | solution.py:103
  98.9 2.8 copy-start
  98.9 2.8 copy-start.3
  103.0 6.3 %copy-start.2 = (bf16[96,4096]{1,0:T(8,128)(2,1)S(1)}, bf16[96,4096]{1,0:T(8,128)(2,1)}, u32[]{:S(2)}) copy-start(bf16[96,4096]{1,0:T(8,128)(2,1)} %copy-done.1) | copy-start | bytes 2359300
  125.3 71.2 %copy-start.4 = (bf16[768,1024]{1,0:T(8,128)(2,1)}, bf16[768,1024]{1,0:T(8,128)(2,1)S(1)}, u32[]{:S(2)}) copy-start(bf16[768,1024]{1,0:T(8,128)(2,1)S(1)} %fusion.4) | copy-start | bytes 4718596
  125.3 3.4 copy-start.9
  126.6 191.8 %all-gather.7.cloned.1.call-start = ((), (), s32[]{:S(2)}) async-start(), calls=%async_computation.2 | async-start | bytes 4325376 | tf_op jit(solution)/shard_map/all_gather | solution.py:143
  127.4 242.2 %reduce-scatter.2.cloned.1.call-start = ((), (), s32[]{:S(2)}) async-start(), calls=%async_computation.3 | async-start | bytes 7077888 | tf_op jit(solution)/shard_map/reduce_scatter | solution.py:144
  315.0 3.5 copy-start.8
Sparse Core Ops, SparseCore 0:
  9.9 101.9 all-gather.4
  126.8 107.0 all-gather.8
  236.3 77.5 all-gather.6
  326.4 43.2 reduce-scatter.1
